TPU v7x, 256 devices: a whole 4x4x8 slice. The times are simulated.
256 devices in a mesh: section: 32 (over z_hi, y, core), fsdp: 8 (over x, z_lo).
Axes of the slice: x: 4, y: 4, z: 8 (z_hi: 4, z_lo: 2; z = z_hi * 2 + z_lo), core: 2. Of those that a mesh axis runs over, the one named last changes fastest.
Arguments:
- acts: bfloat16 [2, 2048, 4096], P(None, 'fsdp'), may hold values from -6 to 6
- gains: float32 [2, 4096], replicated, may hold values from 0.1 to 1.9
- gate_w: bfloat16 [4096, 28672], P('fsdp', 'section'), may hold values from -0.09375 to 0.09375
- up_w: bfloat16 [4096, 28672], P('fsdp', 'section'), may hold values from -0.09375 to 0.09375
- down_w: bfloat16 [28672, 4096], P('section', 'fsdp'), may hold values from -0.046875 to 0.046875
Outputs:
- final_acts: bfloat16 [32, 2048, 4096], P('section', 'fsdp')
All inputs are finite; a program needn't handle non-finite values.
Results may differ from a plain program's by a relative error of at most 0.0047.
Values may be sent and summed in bfloat16 or wider, within the bound.
No kernel may reach another device: no remote copies, remote signals or barrier semaphores. Data moves between devices by JAX's collectives and lax.ppermute only.
A program may use at most 128 MiB of HBM per device.

v0:
```python
import jax
import jax.numpy as jnp
from jax import lax
from jax.sharding import PartitionSpec as P

LAYERS = 2


def swapped(block, axis, stride):
    count = lax.axis_size(axis)
    route = []
    for low in range(count):
        high = low | 1 << stride
        if high != low and high < count:
            route += [(low, high), (high, low)]
    return lax.ppermute(block, axis, route)


def shifted(shard, axis, by):
    length = lax.axis_size(axis)
    return lax.ppermute(shard, axis, [(i, (i + by) % length) for i in range(length)])


def local(acts, gains, gate_w, up_w, down_w):
    group = lax.axis_size("section") // LAYERS
    levels = group.bit_length() - 1
    position = lax.axis_index("section")
    layer = position // group
    state = lax.dynamic_index_in_dim(acts, layer, 0, keepdims=False)
    gain = lax.dynamic_index_in_dim(gains, layer, 0, keepdims=False)
    widened = state.astype(jnp.float32)
    meansq = jnp.mean(widened * widened, axis=-1, keepdims=True)
    normed = (widened * lax.rsqrt(meansq + 1e-05) * gain).astype(jnp.bfloat16)
    gate_panel, up_panel, down_panel = (
        lax.all_gather(gate_w, "fsdp", axis=0, tiled=True),
        lax.all_gather(up_w, "fsdp", axis=0, tiled=True),
        lax.all_gather(down_w, "fsdp", axis=1, tiled=True),
    )
    gate = jnp.dot(normed, gate_panel, preferred_element_type=jnp.float32)
    upper = jnp.dot(normed, up_panel, preferred_element_type=jnp.float32)
    hidden = (jax.nn.silu(gate) * upper).astype(jnp.bfloat16)
    partial_sum = jnp.dot(hidden, down_panel, preferred_element_type=jnp.float32)
    for level in range(levels):
        partial_sum = partial_sum + swapped(partial_sum, "section", level)
    block = (widened + partial_sum).astype(jnp.bfloat16)
    moved = shifted(block, "section", group)
    return moved[None]


def solution(mesh):
    in_specs = (
        P(None, "fsdp", None),
        P(),
        P("fsdp", "section"),
        P("fsdp", "section"),
        P("section", "fsdp"),
    )
    out_specs = P("section", "fsdp", None)
    return jax.shard_map(local, mesh=mesh, in_specs=in_specs, out_specs=out_specs, check_vma=False)
```

profile of v0, /device:TPU:6, one launch (start us, length us, event | category | flops | bytes accessed | tf_op | source)
XLA Modules:
  0.0 968.5 jit_solution(2469996110959038577)
XLA Ops:
  6.5 0.0 copy-start
  6.5 0.0 all-gather.4.cloned.1.call-start
  6.5 0.7 all-gather.4.cloned.1.call-update
  7.3 0.0 all-gather.6.cloned.1.call-start
  7.3 0.7 all-gather.6.cloned.1.call-update
  8.0 0.0 all-gather.8.cloned.1.call-start
  8.1 0.7 all-gather.8.cloned.1.call-update
  8.8 2.1 fusion
  10.9 0.0 copy-done
  10.9 152.5 %all-gather.4.cloned.1.call-done = bf16[4096,896]{1,0:T(8,128)(2,1)} async-done(((bf16[512,896]{1,0:T(8,128)(2,1)}), bf16[4096,896]{1,0:T(8,128)(2,1)}) %all-gather.4.cloned.1.call-update) | async-done | bytes 7340048 | tf_op jit(solution)/shard_map/all_gather | solution.py:35
  163.4 6.1 fusion.9
  169.5 147.9 %all-gather.6.cloned.1.call-done = bf16[4096,896]{1,0:T(8,128)(2,1)} async-done(((bf16[512,896]{1,0:T(8,128)(2,1)}), bf16[4096,896]{1,0:T(8,128)(2,1)}) %all-gather.6.cloned.1.call-update) | async-done | bytes 7340048 | tf_op jit(solution)/shard_map/all_gather | solution.py:36
  317.5 154.1 %all-gather.8.cloned.1.call-done = bf16[896,4096]{1,0:T(8,128)(2,1)} async-done(((bf16[896,512]{1,0:T(8,128)(2,1)}), bf16[896,4096]{1,0:T(8,128)(2,1)}) %all-gather.8.cloned.1.call-update) | async-done | bytes 7340048 | tf_op jit(solution)/shard_map/all_gather | solution.py:37
  471.6 12.4 %fusion.5 = f32[256,4096]{1,0:T(8,128)} fusion(bf16[896,4096]{1,0:T(8,128)(2,1)} %all-gather.8.cloned.1.call-done, bf16[4096,896]{1,0:T(8,128)(2,1)} %all-gather.6.cloned.1.call-done, f32[256,896]{1,0:T(8,128)S(1)} %fusion.9, f32[4096]{0:T(1024)S(1)} %bitcast.15, f32[256]{0:T(256)S(1)} %add_rsqrt_fusion, bf16[2,256,4096]{2,1,0:T(8,128)(2,1)} %param.5, ...), kind=kOutput, calls=%fused_computation.9 | convolution fusion | flops 3763666944 | bytes 21906436 | tf_op jit(solution)/shard_map/dot_general | solution.py:42
  484.0 0.0 collective-permute-start
  484.0 7.4 collective-permute-done
  491.3 2.8 add.41
  494.1 1.6 collective-permute-start.1
  495.7 91.1 %collective-permute-done.1 = f32[256,4096]{1,0:T(8,128)S(1)} collective-permute-done((f32[256,4096]{1,0:T(8,128)S(1)}, f32[256,4096]{1,0:T(8,128)S(1)}, u32[]{:S(2)}, u32[]{:S(2)}) %collective-permute-start.1) | collective-permute-done | bytes 4194336 | tf_op jit(solution)/shard_map/ppermute | solution.py:16
  586.8 0.5 add.42
  587.3 0.0 copy-start.2
  587.3 3.1 collective-permute-start.2
  590.4 90.3 %collective-permute-done.2 = f32[256,4096]{1,0:T(8,128)S(1)} collective-permute-done((f32[256,4096]{1,0:T(8,128)S(1)}, f32[256,4096]{1,0:T(8,128)S(1)}, u32[]{:S(2)}, u32[]{:S(2)}) %collective-permute-start.2) | collective-permute-done | bytes 4194336 | tf_op jit(solution)/shard_map/ppermute | solution.py:16
  680.7 0.6 add.43
  681.3 2.6 collective-permute-start.3
  683.9 178.9 %collective-permute-done.3 = f32[256,4096]{1,0:T(8,128)S(1)} collective-permute-done((f32[256,4096]{1,0:T(8,128)S(1)}, f32[256,4096]{1,0:T(8,128)S(1)}, u32[]{:S(2)}, u32[]{:S(2)}) %collective-permute-start.3) | collective-permute-done | bytes 4194336 | tf_op jit(solution)/shard_map/ppermute | solution.py:16
  862.8 0.0 copy-done.2
  862.8 0.0 copy-start.1
  862.8 1.0 fusion.3
  863.8 5.1 collective-permute-start.4
  868.9 91.7 %collective-permute-done.4 = bf16[256,4096]{1,0:T(8,128)(2,1)S(1)} collective-permute-done((bf16[256,4096]{1,0:T(8,128)(2,1)S(1)}, bf16[256,4096]{1,0:T(8,128)(2,1)S(1)}, u32[]{:S(2)}, u32[]{:S(2)}) %collective-permute-start.4) | collective-permute-done | bytes 2097184 | tf_op jit(solution)/shard_map/ppermute | solution.py:21
  960.6 1.3 copy.7
  961.9 0.0 copy-done.1
  (2 shorter events, 0.0 us)
Async XLA Ops:
  6.5 4.3 copy-start
  6.5 156.9 %all-gather.4.cloned.1.call-start = ((), (), s32[]{:S(2)}) async-start(), calls=%async_computation | async-start | bytes 8257536 | tf_op jit(solution)/shard_map/all_gather | solution.py:35
  7.3 310.2 %all-gather.6.cloned.1.call-start = ((), (), s32[]{:S(2)}) async-start(), calls=%async_computation.1 | async-start | bytes 8257536 | tf_op jit(solution)/shard_map/all_gather | solution.py:36
  8.0 463.5 %all-gather.8.cloned.1.call-start = ((), (), s32[]{:S(2)}) async-start(), calls=%async_computation.2 | async-start | bytes 8257536 | tf_op jit(solution)/shard_map/all_gather | solution.py:37
  484.0 7.4 collective-permute-start
  494.1 92.7 %collective-permute-start.1 = (f32[256,4096]{1,0:T(8,128)S(1)}, f32[256,4096]{1,0:T(8,128)S(1)}, u32[]{:S(2)}, u32[]{:S(2)}) collective-permute-start(f32[256,4096]{1,0:T(8,128)S(1)} %add.41), channel_id=1, source_target_pairs={{0,16},{16,0},{8,24},{24,8},{32,48},{48,32},{40,56},{56,40},{64,80... | collective-permute-start | bytes 12582920 | tf_op jit(solution)/shard_map/ppermute | solution.py:16
  587.3 275.5 %copy-start.2 = (bf16[2,256,4096]{2,1,0:T(8,128)(2,1)S(1)}, bf16[2,256,4096]{2,1,0:T(8,128)(2,1)}, u32[]{:S(2)}) copy-start(bf16[2,256,4096]{2,1,0:T(8,128)(2,1)} %param.5) | copy-start | bytes 12582916
  587.3 93.4 %collective-permute-start.2 = (f32[256,4096]{1,0:T(8,128)S(1)}, f32[256,4096]{1,0:T(8,128)S(1)}, u32[]{:S(2)}, u32[]{:S(2)}) collective-permute-start(f32[256,4096]{1,0:T(8,128)S(1)} %add.42), channel_id=1, source_target_pairs={{0,32},{32,0},{8,40},{40,8},{16,48},{48,16},{24,56},{56,24},{64,96... | collective-permute-start | bytes 12582920 | tf_op jit(solution)/shard_map/ppermute | solution.py:16
  681.3 181.5 %collective-permute-start.3 = (f32[256,4096]{1,0:T(8,128)S(1)}, f32[256,4096]{1,0:T(8,128)S(1)}, u32[]{:S(2)}, u32[]{:S(2)}) collective-permute-start(f32[256,4096]{1,0:T(8,128)S(1)} %add.43), channel_id=1, source_target_pairs={{0,64},{64,0},{8,72},{72,8},{16,80},{80,16},{24,88},{88,24},{32,96... | collective-permute-start | bytes 12582920 | tf_op jit(solution)/shard_map/ppermute | solution.py:16
  862.8 99.1 %copy-start.1 = (f32[2,4096]{1,0:T(2,128)S(1)}, f32[2,4096]{1,0:T(2,128)}, u32[]{:S(2)}) copy-start(f32[2,4096]{1,0:T(2,128)} %param.6) | copy-start | bytes 98308
  863.8 96.8 %collective-permute-start.4 = (bf16[256,4096]{1,0:T(8,128)(2,1)S(1)}, bf16[256,4096]{1,0:T(8,128)(2,1)S(1)}, u32[]{:S(2)}, u32[]{:S(2)}) collective-permute-start(bf16[256,4096]{1,0:T(8,128)(2,1)S(1)} %fusion.3), channel_id=1, source_target_pairs={{0,128},{8,136},{16,144},{24,152},{32,160},{40,168},{48,176},{56,1... | collective-permute-start | bytes 6291464 | tf_op jit(solution)/shard_map/ppermute | solution.py:21
Sparse Core Ops, SparseCore 0:
  9.1 154.2 all-gather.3
  165.2 152.2 all-gather.5
  319.3 152.2 all-gather.7
where the time goes:
time: 969 us; the launch traced here: 968 us
  waiting for transfers between devices  916 us (95%)
  matrix products  18.5 us (2%)
  between operations  13.2 us (1%)
  starting transfers between devices  12.5 us (1%)
    ppermute x4, waiting for transfers between devices, swapped(): return lax.ppermute(block, axis, route)  368 us
    all_gather x1, waiting for transfers between devices, local(): lax.all_gather(down_w, 'fsdp', axis=1, tiled=True)  154 us
    all_gather x1, waiting for transfers between devices, local(): lax.all_gather(gate_w, 'fsdp', axis=0, tiled=True)  153 us
    all_gather x1, waiting for transfers between devices, local(): lax.all_gather(up_w, 'fsdp', axis=0, tiled=True)  148 us
    ppermute x1, waiting for transfers between devices, shifted(): lax.ppermute(shard, axis, [(i, (i + by) % length) for i in range(length)])  91.7 us
  transfers between devices with their start and end apart: 8, of which 8 were waited for; matrix products, arithmetic and copies ran while one was open for 1% of the time, Pallas kernels for 0%

commit v1 on v0

--- a/solution.py
+++ b/solution.py
@@ -33,7 +33,9 @@
     normed = (widened * lax.rsqrt(meansq + 1e-05) * gain).astype(jnp.bfloat16)
     gate_panel, up_panel, down_panel = (
         lax.all_gather(gate_w, "fsdp", axis=0, tiled=True),
-        lax.all_gather(up_w, "fsdp", axis=0, tiled=True),
+        jnp.concatenate(
+            lax.all_to_all(jnp.stack([up_w] * lax.axis_size("fsdp")), "fsdp", 0, 0), axis=0
+        ),
         lax.all_gather(down_w, "fsdp", axis=1, tiled=True),
     )
     gate = jnp.dot(normed, gate_panel, preferred_element_type=jnp.float32)

time: 969 us -> 890 us (0.918)
  waiting for transfers between devices: 916 us -> 825 us
    all_gather x1 -> x0, waiting for transfers between devices: 148 us -> none  [local(): lax.all_gather(up_w, 'fsdp', axis=0, tiled=True)]
    all_gather x1, waiting for transfers between devices: 153 us -> 215 us  [local(): lax.all_gather(gate_w, 'fsdp', axis=0, tiled=True)]
  transfers between devices with their start and end apart: 8 -> 8, of which waited for: 8 -> 7; matrix products, arithmetic and copies ran while one was open for 1% -> 1% of each run, Pallas kernels for 0% -> 0%
where the time goes in v1:
time: 890 us
  waiting for transfers between devices  825 us (93%)
  starting transfers between devices  19.4 us (2%)
  matrix products  18.5 us (2%)
  between operations  13.5 us (2%)
    ppermute x4, waiting for transfers between devices, swapped(): return lax.ppermute(block, axis, route)  368 us
    all_gather x1, waiting for transfers between devices, local(): lax.all_gather(gate_w, 'fsdp', axis=0, tiled=True)  215 us
    all_gather x1, waiting for transfers between devices, local(): lax.all_gather(down_w, 'fsdp', axis=1, tiled=True)  149 us
    ppermute x1, waiting for transfers between devices, shifted(): lax.ppermute(shard, axis, [(i, (i + by) % length) for i in range(length)])  91.7 us
  transfers between devices with their start and end apart: 8, of which 7 were waited for; matrix products, arithmetic and copies ran while one was open for 1% of the time, Pallas kernels for 0%

profile of v1, /device:TPU:6, one launch (start us, length us, event | category | flops | bytes accessed | tf_op | source)
XLA Modules:
  0.0 889.8 jit_solution(10779722085936495110)
XLA Ops:
  6.5 0.0 copy-start
  6.5 0.0 all-gather.3.cloned.1.call-start
  6.5 0.7 all-gather.3.cloned.1.call-update
  7.3 5.1 stack.2
  12.3 7.0 all-to-all-start
  19.3 0.0 all-gather.5.cloned.1.call-start
  19.3 0.7 all-gather.5.cloned.1.call-update
  20.1 2.1 fusion.3
  22.1 0.0 copy-done
  22.2 214.9 %all-gather.3.cloned.1.call-done = bf16[4096,896]{1,0:T(8,128)(2,1)} async-done(((bf16[512,896]{1,0:T(8,128)(2,1)}), bf16[4096,896]{1,0:T(8,128)(2,1)}) %all-gather.3.cloned.1.call-update) | async-done | bytes 7340048 | tf_op jit(solution)/shard_map/all_gather | solution.py:35
  237.1 6.1 fusion.12
  243.2 0.0 all-to-all-done
  243.3 149.3 %all-gather.5.cloned.1.call-done = bf16[896,4096]{1,0:T(8,128)(2,1)} async-done(((bf16[896,512]{1,0:T(8,128)(2,1)}), bf16[896,4096]{1,0:T(8,128)(2,1)}) %all-gather.5.cloned.1.call-update) | async-done | bytes 7340048 | tf_op jit(solution)/shard_map/all_gather | solution.py:39
  392.6 12.4 %fusion.27 = f32[256,4096]{1,0:T(8,128)} fusion(bf16[896,4096]{1,0:T(8,128)(2,1)} %all-gather.5.cloned.1.call-done, bf16[4096,896]{1,0:T(8,128)(2,1)} %bitcast.3, f32[4096]{0:T(1024)S(1)} %bitcast.34, f32[256]{0:T(256)S(1)} %add_rsqrt_fusion, bf16[2,256,4096]{2,1,0:T(8,128)(2,1)} %param.5, s32[]{:T(128)S(6)} %select_n.12, f32[256,896]{1,0:T(8,128)S(1)} %fusion.12), kind=kOutput, calls=%fused_computation.22 | convolution fusion | flops 3763666944 | bytes 21906436 | tf_op jit(solution)/shard_map/dot_general | solution.py:44
  405.0 0.0 collective-permute-start
  405.0 7.4 collective-permute-done
  412.4 2.8 add.41
  415.1 1.6 collective-permute-start.1
  416.7 91.1 %collective-permute-done.1 = f32[256,4096]{1,0:T(8,128)S(1)} collective-permute-done((f32[256,4096]{1,0:T(8,128)S(1)}, f32[256,4096]{1,0:T(8,128)S(1)}, u32[]{:S(2)}, u32[]{:S(2)}) %collective-permute-start.1) | collective-permute-done | bytes 4194336 | tf_op jit(solution)/shard_map/ppermute | solution.py:16
  507.8 0.5 add.42
  508.3 0.0 copy-start.2
  508.3 3.1 collective-permute-start.2
  511.5 90.3 %collective-permute-done.2 = f32[256,4096]{1,0:T(8,128)S(1)} collective-permute-done((f32[256,4096]{1,0:T(8,128)S(1)}, f32[256,4096]{1,0:T(8,128)S(1)}, u32[]{:S(2)}, u32[]{:S(2)}) %collective-permute-start.2) | collective-permute-done | bytes 4194336 | tf_op jit(solution)/shard_map/ppermute | solution.py:16
  601.7 0.6 add.43
  602.3 2.6 collective-permute-start.3
  604.9 178.9 %collective-permute-done.3 = f32[256,4096]{1,0:T(8,128)S(1)} collective-permute-done((f32[256,4096]{1,0:T(8,128)S(1)}, f32[256,4096]{1,0:T(8,128)S(1)}, u32[]{:S(2)}, u32[]{:S(2)}) %collective-permute-start.3) | collective-permute-done | bytes 4194336 | tf_op jit(solution)/shard_map/ppermute | solution.py:16
  783.8 0.0 copy-done.2
  783.8 0.0 copy-start.1
  783.8 1.0 fusion.6
  784.8 5.1 collective-permute-start.4
  789.9 91.7 %collective-permute-done.4 = bf16[256,4096]{1,0:T(8,128)(2,1)S(1)} collective-permute-done((bf16[256,4096]{1,0:T(8,128)(2,1)S(1)}, bf16[256,4096]{1,0:T(8,128)(2,1)S(1)}, u32[]{:S(2)}, u32[]{:S(2)}) %collective-permute-start.4) | collective-permute-done | bytes 2097184 | tf_op jit(solution)/shard_map/ppermute | solution.py:21
  881.7 1.3 copy.7
  883.0 0.0 copy-done.1
  (2 shorter events, 0.0 us)
Async XLA Ops:
  6.5 15.6 %copy-start = (f32[2,4096]{1,0:T(2,128)S(1)}, f32[2,4096]{1,0:T(2,128)}, u32[]{:S(2)}) copy-start(f32[2,4096]{1,0:T(2,128)} %param.6) | copy-start | bytes 98308
  6.5 230.6 %all-gather.3.cloned.1.call-start = ((), (), s32[]{:S(2)}) async-start(), calls=%async_computation.1 | async-start | bytes 8257536 | tf_op jit(solution)/shard_map/all_gather | solution.py:35
  12.3 230.9 %all-to-all-start = ((bf16[8,512,896]{2,1,0:T(8,128)(2,1)}), bf16[8,512,896]{2,1,0:T(8,128)(2,1)}, u32[]{:S(2)}, u32[]{:S(2)}) async-start(bf16[8,512,896]{2,1,0:T(8,128)(2,1)} %stack.2), calls=%async_computation | async-start | bytes 14680064 | tf_op jit(solution)/shard_map/all_to_all | solution.py:37
  19.3 373.3 %all-gather.5.cloned.1.call-start = ((), (), s32[]{:S(2)}) async-start(), calls=%async_computation.2 | async-start | bytes 8257536 | tf_op jit(solution)/shard_map/all_gather | solution.py:39
  405.0 7.4 collective-permute-start
  415.1 92.7 %collective-permute-start.1 = (f32[256,4096]{1,0:T(8,128)S(1)}, f32[256,4096]{1,0:T(8,128)S(1)}, u32[]{:S(2)}, u32[]{:S(2)}) collective-permute-start(f32[256,4096]{1,0:T(8,128)S(1)} %add.41), channel_id=1, source_target_pairs={{0,16},{16,0},{8,24},{24,8},{32,48},{48,32},{40,56},{56,40},{64,80... | collective-permute-start | bytes 12582920 | tf_op jit(solution)/shard_map/ppermute | solution.py:16
  508.3 275.5 %copy-start.2 = (bf16[2,256,4096]{2,1,0:T(8,128)(2,1)S(1)}, bf16[2,256,4096]{2,1,0:T(8,128)(2,1)}, u32[]{:S(2)}) copy-start(bf16[2,256,4096]{2,1,0:T(8,128)(2,1)} %param.5) | copy-start | bytes 12582916
  508.3 93.4 %collective-permute-start.2 = (f32[256,4096]{1,0:T(8,128)S(1)}, f32[256,4096]{1,0:T(8,128)S(1)}, u32[]{:S(2)}, u32[]{:S(2)}) collective-permute-start(f32[256,4096]{1,0:T(8,128)S(1)} %add.42), channel_id=1, source_target_pairs={{0,32},{32,0},{8,40},{40,8},{16,48},{48,16},{24,56},{56,24},{64,96... | collective-permute-start | bytes 12582920 | tf_op jit(solution)/shard_map/ppermute | solution.py:16
  602.3 181.5 %collective-permute-start.3 = (f32[256,4096]{1,0:T(8,128)S(1)}, f32[256,4096]{1,0:T(8,128)S(1)}, u32[]{:S(2)}, u32[]{:S(2)}) collective-permute-start(f32[256,4096]{1,0:T(8,128)S(1)} %add.43), channel_id=1, source_target_pairs={{0,64},{64,0},{8,72},{72,8},{16,80},{80,16},{24,88},{88,24},{32,96... | collective-permute-start | bytes 12582920 | tf_op jit(solution)/shard_map/ppermute | solution.py:16
  783.8 99.1 %copy-start.1 = (f32[2,4096]{1,0:T(2,128)S(1)}, f32[2,4096]{1,0:T(2,128)}, u32[]{:S(2)}) copy-start(f32[2,4096]{1,0:T(2,128)} %param.6) | copy-start | bytes 98308
  784.8 96.8 %collective-permute-start.4 = (bf16[256,4096]{1,0:T(8,128)(2,1)S(1)}, bf16[256,4096]{1,0:T(8,128)(2,1)S(1)}, u32[]{:S(2)}, u32[]{:S(2)}) collective-permute-start(bf16[256,4096]{1,0:T(8,128)(2,1)S(1)} %fusion.6), channel_id=1, source_target_pairs={{0,128},{8,136},{16,144},{24,152},{32,160},{40,168},{48,176},{56,1... | collective-permute-start | bytes 6291464 | tf_op jit(solution)/shard_map/ppermute | solution.py:21
Sparse Core Ops, SparseCore 0:
  9.1 227.9 all-gather.2
  238.9 153.6 all-gather.4
